TPU v7x, 32 devices: a whole 2x2x4 slice. The times are simulated.
32 devices in a mesh: clip: 2 (over x), slab: 16 (over z, y, core).
Axes of the slice: x: 2, y: 2, z: 4, core: 2. Of those that a mesh axis runs over, the one named last changes fastest.
Arguments:
- mask_field: float32 [4096, 2048], P(('clip', 'slab')), parts along dimension 0, may hold values from -1.8 to 2.9
- target_print: int32 [4096, 2048], P(('clip', 'slab')), parts along dimension 0, may hold values from 0 to 1
- source_points: int32 [32, 2], P('clip'), parts along dimension 0, may hold values from 0 to 60
- source_groups: int32 [32], P('clip'), parts along dimension 0, may hold values from 0 to 7
- group_logits: float32 [16], P('clip'), parts along dimension 0, may hold values from -1 to 1
- pupil_radius: int32 [2], P('clip'), parts along dimension 0, may hold values from 32 to 127
Outputs:
- loss_value: float32 [2], P('clip'), parts along dimension 0
- mask_grad: float32 [4096, 2048], P(('clip', 'slab')), parts along dimension 0
- group_grad: float32 [16], P('clip'), parts along dimension 0
There are 2 independent parts, one for each index of `clip`. A program takes and returns all parts, laid end to end along the dimension named above; each array names one. Nothing has to cross between parts.
All inputs are finite; a program needn't handle non-finite values.
Results may differ from a plain program's by a relative error of at most 0.0003.
Values sent between devices are 32-bit elements; how exact they have to be, the bound alone decides.
A program may use at most 128 MiB of HBM per device.

v0:
```python
import math

import jax
import jax.numpy as jnp
from jax import lax
from jax.sharding import PartitionSpec as P

K = 256
GRID = 61
NG = 8


steepness = 8.0
threshold = 0.3
shift_scale = 45
full_turn = 2.0 * math.pi
highest = lax.Precision.HIGHEST


def contract(form, left, right):
    return jnp.einsum(form, left, right, precision=highest)


def turn_table(left, right, length):
    product = jnp.mod(left[:, None] * right[None, :], length)
    angles = full_turn * product.astype(jnp.float32) / length
    return (jnp.cos(angles), jnp.sin(angles))


def pupil_mask(shifted, radius_sq, along_first, along_second):
    first_axis = along_first[None, :, None] + shifted[:, 0, None, None]
    second_axis = along_second[None, None, :] + shifted[:, 1, None, None]
    return (first_axis * first_axis + second_axis * second_axis <= radius_sq).astype(jnp.float32)


def on_device(mask_field, target_print, source_points, source_groups, group_logits, pupil_radius):
    row_count = mask_field.shape[0]
    length = mask_field.shape[1]
    half_band = K // 2
    device = lax.axis_index("slab")
    positions = device * row_count + jnp.arange(row_count, dtype=jnp.int32)
    everywhere = jnp.arange(length, dtype=jnp.int32)
    frequency = jnp.arange(K, dtype=jnp.int32) - half_band
    cos_full, sin_full = turn_table(everywhere, frequency, length)
    cos_local, sin_local = turn_table(positions, frequency, length)
    cutoff = pupil_radius[0]
    radius_sq = cutoff * cutoff
    shifted = (source_points - GRID // 2) * cutoff // shift_scale
    norming = 1.0 / (length * length)
    row_real = jnp.dot(mask_field, cos_full, precision=highest)
    row_imag = -jnp.dot(mask_field, sin_full, precision=highest)
    spec_real = contract("xk,xj->kj", cos_local, row_real) + contract(
        "xk,xj->kj", sin_local, row_imag
    )
    spec_imag = contract("xk,xj->kj", cos_local, row_imag) - contract(
        "xk,xj->kj", sin_local, row_real
    )
    whole_band = lax.psum(jnp.stack([spec_real, spec_imag], 0), "slab")
    width_here = whole_band.shape[2]
    columns = jnp.arange(width_here, dtype=jnp.int32) - half_band
    passed = pupil_mask(shifted, radius_sq, frequency, columns)
    real_part = passed * whole_band[0][None]
    imag_part = passed * whole_band[1][None]
    lifted_real = contract("xk,skj->sxj", cos_local, real_part) - contract(
        "xk,skj->sxj", sin_local, imag_part
    )
    lifted_imag = contract("xk,skj->sxj", cos_local, imag_part) + contract(
        "xk,skj->sxj", sin_local, real_part
    )
    lifted = jnp.stack([lifted_real, lifted_imag], 1)
    field_real = (
        contract("sxk,yk->sxy", lifted[:, 0], cos_full)
        - contract("sxk,yk->sxy", lifted[:, 1], sin_full)
    ) * norming
    field_imag = (
        contract("sxk,yk->sxy", lifted[:, 0], sin_full)
        + contract("sxk,yk->sxy", lifted[:, 1], cos_full)
    ) * norming
    bright = field_real * field_real + field_imag * field_imag
    onehot_table = (source_groups[:, None] == jnp.arange(NG, dtype=jnp.int32)[None, :]).astype(
        jnp.float32
    )
    weights = jnp.exp(jnp.sum(onehot_table * group_logits[None, :], 1))
    total_weight = jnp.sum(weights)
    weight_share = weights / total_weight
    intensity = jnp.einsum("s,sxy->xy", weight_share, bright, precision=highest)
    resist = jax.nn.sigmoid(steepness * (intensity - threshold))
    misfit = resist - target_print.astype(jnp.float32)
    slope_map = 2.0 * misfit * steepness * resist * (1.0 - resist)
    per_source = contract("sxy,xy->s", bright, slope_map)
    against = jnp.sum(slope_map * intensity)
    squares = jnp.sum(misfit * misfit)
    per_source, against, squares = lax.psum((per_source, against, squares), "slab")
    loss_value = (squares * norming).reshape(1)
    source_pull = weights * (per_source - against) / total_weight
    group_grad = jnp.sum(onehot_table * source_pull[:, None], 0) * norming
    factor = 2.0 * weight_share[:, None, None] * slope_map[None] * norming
    back_real = factor * field_real
    back_imag = factor * field_imag
    down_real = contract("sxy,yk->sxk", back_real, cos_full) + contract(
        "sxy,yk->sxk", back_imag, sin_full
    )
    down_imag = contract("sxy,yk->sxk", back_imag, cos_full) - contract(
        "sxy,yk->sxk", back_real, sin_full
    )
    settle_real = contract("xk,sxj->skj", cos_local, down_real) + contract(
        "xk,sxj->skj", sin_local, down_imag
    )
    settle_imag = contract("xk,sxj->skj", cos_local, down_imag) - contract(
        "xk,sxj->skj", sin_local, down_real
    )
    passed = pupil_mask(shifted, radius_sq, frequency, frequency)
    pull_band = jnp.stack([jnp.sum(passed * settle_real, 0), jnp.sum(passed * settle_imag, 0)], 0)
    whole_pull = lax.psum(pull_band, "slab")
    spread_real = contract("xk,kj->xj", cos_local, whole_pull[0]) - contract(
        "xk,kj->xj", sin_local, whole_pull[1]
    )
    spread_imag = contract("xk,kj->xj", cos_local, whole_pull[1]) + contract(
        "xk,kj->xj", sin_local, whole_pull[0]
    )
    spread_out = jnp.stack([spread_real, spread_imag], 0)
    mask_grad = contract("xk,yk->xy", spread_out[0], cos_full) - contract(
        "xk,yk->xy", spread_out[1], sin_full
    )
    return (loss_value, mask_grad, group_grad)


def solution(mesh):
    in_specs = (
        P(("clip", "slab"), None),
        P(("clip", "slab"), None),
        P("clip", None),
        P("clip"),
        P("clip"),
        P("clip"),
    )
    out_specs = (P("clip"), P(("clip", "slab"), None), P("clip"))
    return jax.shard_map(
        on_device, mesh=mesh, in_specs=in_specs, out_specs=out_specs, check_vma=False
    )
```

profile of v0, /device:TPU:0, one launch (start us, length us, event | category | flops | bytes accessed | tf_op | source)
XLA Modules:
  0.0 627.9 jit_solution(16755961232208500277)
XLA Ops:
  7.2 1.2 copy-done
  8.4 10.9 %convolution_negate_fusion = f32[256,128]{1,0:T(8,128)S(1)} fusion(f32[128,2048]{1,0:T(8,128)S(1)} %copy-done, s32[256]{0:T(256)S(1)} %iota_add_fusion), kind=kOutput, calls=%fused_computation.93 | convolution fusion | flops 812679168 | bytes 1180672 | tf_op jit(solution)/shard_map/dot_general | solution.py:51
  19.4 11.1 %fusion.112 = f32[256,128]{1,0:T(8,128)S(1)} fusion(f32[128,2048]{1,0:T(8,128)S(1)} %copy-done, s32[256]{0:T(256)S(1)} %iota_add_fusion), kind=kOutput, calls=%fused_computation.110 | convolution fusion | flops 812646400 | bytes 1180672 | tf_op jit(solution)/shard_map/dot_general | solution.py:50
  30.5 0.9 fusion.145
  31.4 1.2 fusion.143
  32.6 0.9 fusion.93
  33.5 0.9 fusion.92
  34.5 0.8 pad_maximum_fusion
  35.3 0.0 all-reduce.6.cloned.1.call-start
  36.1 0.1 select_reduce_fusion.1
  36.2 0.6 exponential_reduce_fusion
  36.8 0.1 add_multiply_fusion.2
  36.9 92.1 %all-reduce.4.cloned.1.call-done = f32[2,256,256]{2,1,0:T(8,128)} async-done(((f32[2,256,256]{2,1,0:T(8,128)}), f32[2,256,256]{2,1,0:T(8,128)}) %all-reduce.4.cloned.1.call-update) | async-done | bytes 524304 | tf_op jit(solution)/shard_map/psum | solution.py:58
  129.0 1.1 slice_bitcast_fusion.3
  130.1 0.1 copy.30
  130.2 4.0 fusion.26
  134.2 5.4 fusion.28
  139.6 0.1 copy.29
  139.7 6.1 fusion.76
  145.8 37.3 %fusion.41 = f32[16,128,2048]{2,1,0:T(8,128)} fusion(f32[16,256,128]{2,1,0:T(8,128)S(1)} %fusion.76, s32[256]{0:T(256)S(1)} %iota_add_fusion), kind=kOutput, calls=%fused_computation.48 | convolution fusion | flops 12892241920 | bytes 18875392 | tf_op jit(solution)/shard_map/sxk,yk->sxy/dot_general | solution.py:21
  183.2 36.5 %fusion.49 = f32[16,128,2048]{2,1,0:T(8,128)S(1)} fusion(f32[16,256,128]{2,1,0:T(8,128)S(1)} %fusion.76, s32[256]{0:T(256)S(1)} %iota_add_fusion), kind=kOutput, calls=%fused_computation.56 | convolution fusion | flops 12892241920 | bytes 18875392 | tf_op jit(solution)/shard_map/sxk,yk->sxy/dot_general | solution.py:21
  219.7 4.1 fusion.79
  223.9 1.3 copy-done.2
  225.2 38.2 %subtract_multiply_fusion = f32[16,128,2048]{2,1,0:T(8,128)} fusion(f32[16,128,2048]{2,1,0:T(8,128)S(1)} %fusion.49, f32[16,256,128]{2,1,0:T(8,128)S(1)} %fusion.79, s32[256]{0:T(256)S(1)} %iota_add_fusion), kind=kOutput, calls=%fused_computation.5 | convolution fusion | flops 12900630528 | bytes 35652608 | tf_op jit(solution)/shard_map/sxk,yk->sxy/dot_general | solution.py:21
  263.4 43.0 %multiply_add_fusion = (f32[16,128,2048]{2,1,0:T(8,128)S(1)}, f32[16,128,2048]{2,1,0:T(8,128)}) fusion(f32[16,128,2048]{2,1,0:T(8,128)} %subtract_multiply_fusion, f32[16,128,2048]{2,1,0:T(8,128)} %fusion.41, s32[256]{0:T(256)S(1)} %iota_add_fusion, f32[16,256,128]{2,1,0:T(8,128)} %copy-done.2), kind=kOutput, calls=%fused_computation.3 | convolution fusion | flops 12913213440 | bytes 69207040 | tf_op jit(solution)/shard_map/sxk,yk->sxy/dot_general | solution.py:21
  306.4 17.7 %fusion.4 = f32[1,128,2048]{2,0,1:T(1,128)S(1)} fusion(f32[16,128,2048]{2,1,0:T(8,128)S(1)} %get-tuple-element.17, f32[]{:T(128)} %exponential_reduce_fusion, f32[16]{0:T(128)S(1)} %select_reduce_fusion.1), kind=kOutput, calls=%fused_computation.8 | convolution fusion | flops 50331664 | bytes 17825860 | tf_op jit(solution)/shard_map/s,sxy->xy/dot_general | solution.py:86
  324.1 1.5 fusion.102
  325.6 25.5 %fusion.94 = f32[16]{0:T(128)} fusion(f32[16,128,2048]{2,1,0:T(8,128)S(1)} %get-tuple-element.17, f32[128,2048,1]{1,0,2:T(8,128)S(1)} %bitcast.127), kind=kOutput, calls=%fused_computation.94 | convolution fusion | flops 50331648 | bytes 17825856 | tf_op jit(solution)/shard_map/sxy,xy->s/dot_general | solution.py:21
  351.1 32.7 %all-reduce = (f32[]{:T(128)}, f32[16]{0:T(128)S(1)}, f32[]{:T(128)}) all-reduce(f32[]{:T(128)} %get-tuple-element.4, f32[16]{0:T(128)} %fusion.94, f32[]{:T(128)} %get-tuple-element.3), channel_id=1, replica_groups=mesh['clip'=2,'slab'=16] {'slab'}, use_global_device_ids=true, to_apply=%region_4.5 | all-reduce | flops 18 | bytes 144 | tf_op jit(solution)/shard_map/psum | solution.py:93
  383.8 1.3 multiply_divide_fusion
  385.1 25.5 %fusion.6 = f32[16,128,256]{2,1,0:T(8,128)S(1)} fusion(f32[16,128,2048]{2,1,0:T(8,128)} %subtract_multiply_fusion, f32[128,2048]{1,0:T(8,128)S(1)} %get-tuple-element.8, f32[16]{0:T(128)S(1)} %get-tuple-element.16, s32[256]{0:T(256)S(1)} %iota_add_fusion), kind=kOutput, calls=%fused_computation.10 | convolution fusion | flops 12904824832 | bytes 19924032 | tf_op jit(solution)/shard_map/sxy,yk->sxk/dot_general | solution.py:21
  410.6 24.6 %fusion.8 = f32[16,128,256]{2,1,0:T(8,128)S(1)} fusion(f32[16,128,2048]{2,1,0:T(8,128)} %subtract_multiply_fusion, f32[128,2048]{1,0:T(8,128)S(1)} %get-tuple-element.8, f32[16]{0:T(128)S(1)} %get-tuple-element.16, s32[256]{0:T(256)S(1)} %iota_add_fusion), kind=kOutput, calls=%fused_computation.11 | convolution fusion | flops 12904824832 | bytes 19924032 | tf_op jit(solution)/shard_map/sxy,yk->sxk/dot_general | solution.py:21
  435.2 24.9 %fusion.82 = f32[16,128,256]{2,1,0:T(8,128)S(1)} fusion(f32[16,128,256]{2,1,0:T(8,128)S(1)} %fusion.8, f32[16,128,2048]{2,1,0:T(8,128)} %get-tuple-element.18, f32[128,2048]{1,0:T(8,128)S(1)} %get-tuple-element.8, f32[16]{0:T(128)S(1)} %get-tuple-element.16, s32[256]{0:T(256)S(1)} %iota_add_fusion), kind=kOutput, calls=%fused_computation.85 | convolution fusion | flops 12905349120 | bytes 22021184 | tf_op jit(solution)/shard_map/sxy,yk->sxk/dot_general | solution.py:21
  460.1 25.3 %fusion.87 = f32[16,128,256]{2,1,0:T(8,128)S(1)} fusion(f32[16,128,256]{2,1,0:T(8,128)S(1)} %fusion.6, f32[16,128,2048]{2,1,0:T(8,128)} %get-tuple-element.18, f32[128,2048]{1,0:T(8,128)S(1)} %get-tuple-element.8, f32[16]{0:T(128)S(1)} %get-tuple-element.16, s32[256]{0:T(256)S(1)} %iota_add_fusion), kind=kOutput, calls=%fused_computation.86 | convolution fusion | flops 12905349120 | bytes 22021184 | tf_op jit(solution)/shard_map/sxy,yk->sxk/dot_general | solution.py:21
  485.5 4.2 fusion.129
  489.6 4.2 fusion.131
  493.8 5.2 fusion.34
  499.1 5.1 fusion.35
  504.2 0.8 pad_maximum_fusion.1
  505.0 0.1 select_reduce_fusion
  505.8 0.5 broadcast_multiply_fusion
  506.3 86.8 %all-reduce.6.cloned.1.call-done = f32[2,256,256]{1,2,0:T(8,128)} async-done(((f32[2,256,256]{1,2,0:T(8,128)}), f32[2,256,256]{1,2,0:T(8,128)}) %all-reduce.6.cloned.1.call-update) | async-done | bytes 524304 | tf_op jit(solution)/shard_map/psum | solution.py:114
  593.2 1.8 fusion.120
  595.0 1.8 convolution_subtract_fusion.2
  596.8 9.6 %fusion.109 = f32[128,2048]{1,0:T(8,128)S(1)} fusion(f32[128,256]{1,0:T(8,128)S(1)} %convolution_subtract_fusion.2, s32[256]{0:T(256)S(1)} %iota_add_fusion), kind=kOutput, calls=%fused_computation.109 | convolution fusion | flops 812646400 | bytes 1180672 | tf_op jit(solution)/shard_map/xk,yk->xy/dot_general | solution.py:21
  606.4 0.9 fusion.121
  607.3 0.9 convolution_add_fusion.1
  608.2 11.5 %convolution_subtract_fusion = f32[128,2048]{1,0:T(8,128)} fusion(f32[128,2048]{1,0:T(8,128)S(1)} %fusion.109, f32[128,256]{1,0:T(8,128)S(1)} %convolution_add_fusion.1, s32[256]{0:T(256)S(1)} %iota_add_fusion), kind=kOutput, calls=%fused_computation.42 | convolution fusion | flops 812908544 | bytes 2229248 | tf_op jit(solution)/shard_map/xk,yk->xy/dot_general | solution.py:21
  (31 shorter events, 0.2 us)
Async XLA Ops:
  7.2 1.2 copy-start
  7.2 121.8 %all-reduce.4.cloned.1.call-start = ((), (), s32[]{:S(2)}) async-start(), calls=%async_computation | async-start | bytes 1048576 | tf_op jit(solution)/shard_map/psum | solution.py:58
  30.4 5.6 copy-start.8
  30.4 5.7 copy-start.10
  30.4 5.7 copy-start.11
  35.3 557.8 %all-reduce.6.cloned.1.call-start = ((), (), s32[]{:S(2)}) async-start(), calls=%async_computation.1 | async-start | bytes 1048576 | tf_op jit(solution)/shard_map/psum | solution.py:114
  36.9 182.8 %copy-start.4 = (s32[16,256]{1,0:T(8,128)}, s32[16,256]{1,0:T(8,128)S(1)}, u32[]{:S(2)}) copy-start(s32[16,256]{1,0:T(8,128)S(1)} %get-tuple-element.11) | copy-start | bytes 49156
  36.9 182.8 %copy-start.6 = (s32[16,256]{1,0:T(8,128)}, s32[16,256]{1,0:T(8,128)S(1)}, u32[]{:S(2)}) copy-start(s32[16,256]{1,0:T(8,128)S(1)} %get-tuple-element.12) | copy-start | bytes 49156
  223.9 1.3 copy-start.2
  306.4 17.7 %copy-start.3 = (s32[128,2048]{1,0:T(8,128)S(1)}, s32[128,2048]{1,0:T(8,128)}, u32[]{:S(2)}) copy-start(s32[128,2048]{1,0:T(8,128)} %param.7) | copy-start | bytes 3145732
  489.6 4.2 copy-start.5
  489.6 4.2 copy-start.7
  499.1 5.9 copy-start.12
  596.8 9.6 %copy-start.9 = (f32[2,256,256]{1,2,0:T(8,128)S(1)}, f32[2,256,256]{1,2,0:T(8,128)}, u32[]{:S(2)}) copy-start(f32[2,256,256]{1,2,0:T(8,128)} %all-reduce.6.cloned.1.call-done) | copy-start | bytes 1572868
  608.2 11.5 %copy-start.1 = (f32[128,2048]{1,0:T(8,128)S(1)}, f32[128,2048]{1,0:T(8,128)}, u32[]{:S(2)}) copy-start(f32[128,2048]{1,0:T(8,128)} %param.6) | copy-start | bytes 3145732
Sparse Core Ops, SparseCore 0:
  35.5 93.4 all-reduce.3
  505.1 88.0 all-reduce.5
where the time goes:
time: 637 us; the launch traced here: 628 us
  matrix products  389 us (61%)
  waiting for transfers between devices  179 us (28%)
  blocking collectives  32.7 us (5%)
  between operations  17.1 us (3%)
    dot_general x27, matrix products, contract(): return jnp.einsum(form, left, right, precision=highest)  350 us
    psum x1, waiting for transfers between devices, on_device(): whole_band = lax.psum(jnp.stack([spec_real, spec_imag], 0), 'slab')  92.1 us
    psum x1, waiting for transfers between devices, on_device(): whole_pull = lax.psum(pull_band, 'slab')  86.8 us
    psum x1, blocking collectives, on_device(): lax.psum((per_source, against, squares), 'slab')  32.7 us
    dot_general x1, matrix products, on_device(): intensity = jnp.einsum('s,sxy->xy', weight_share, bright, precision=highest)  17.7 us
  transfers between devices with their start and end apart: 2, of which 2 were waited for; matrix products, arithmetic and copies ran while one was open for 0% of the time, Pallas kernels for 0%

commit v1 on v0

v1 whole, which is shorter than its diff:
```python
import functools
import math

import jax
import jax.numpy as jnp
import numpy as np
from jax import lax
from jax.sharding import PartitionSpec as P

K = 256
GRID = 61
NG = 8

steepness = 8.0
threshold = 0.3
shift_scale = 45
HIGH = lax.Precision.HIGH


def dot(form, left, right):
    return jnp.einsum(form, left, right, precision=HIGH, preferred_element_type=jnp.float32)


def waves(left, right, length):
    turns = np.mod(np.asarray(left)[:, None] * np.asarray(right)[None, :], length)
    angles = 2.0 * math.pi * turns.astype(np.float64) / length
    return np.cos(angles), np.sin(angles)


def turned(first, second):
    return (
        first[0] * second[0] - first[1] * second[1],
        first[1] * second[0] + first[0] * second[1],
    )


def shifted_waves(count, freq, length, device, devices):
    near = np.stack(waves(np.arange(count), freq, length)).astype(np.float32)
    far = np.stack(waves(np.arange(devices) * count, freq, length)).astype(np.float32)
    far = lax.dynamic_slice_in_dim(jnp.asarray(far), device, 1, axis=1)
    return turned((far[0], far[1]), (jnp.asarray(near[0]), jnp.asarray(near[1])))


def on_device(devices, mask_field, target_print, source_points, source_groups, group_logits, pupil_radius):
    rows, n = mask_field.shape
    sources = source_points.shape[0]
    coarse = 2 * K
    step = n // coarse
    cols = coarse // devices
    half = n // 2
    device = lax.axis_index("slab")
    freq = np.arange(K, dtype=np.int64) - K // 2
    order = np.concatenate([freq[freq % 2 == 0], freq[freq % 2 == 1]])
    kh = K // 2
    norming = 1.0 / (n * n)

    cos_y, sin_y = waves(np.arange(half), order, n)
    fold = [
        jnp.asarray(np.concatenate([t[:, p * kh : (p + 1) * kh] for t in (cos_y, sin_y)], 1), jnp.float32)
        for p in (0, 1)
    ]
    lag = np.mod(np.arange(n)[None, :] - step * np.arange(coarse // 4)[:, None], n)
    kernel = np.zeros(n)
    for f in range(1, K):
        kernel += 2.0 * np.cos(2.0 * math.pi * np.mod(f * np.arange(n), n) / n)
    kernel = (kernel + 1.0) / coarse
    quarter = lax.optimization_barrier(jnp.asarray(kernel[lag], jnp.float32))
    up = jnp.concatenate([jnp.roll(quarter, i * (n // 4), axis=1) for i in range(4)], 0)
    cos_c, sin_c = waves(freq, np.arange(coarse), coarse)
    wave_x = jnp.asarray(np.concatenate([cos_c, sin_c], 1), jnp.float32)
    loc_c, loc_s = shifted_waves(rows, freq, n, device, devices)
    loc = jnp.concatenate([loc_c, loc_s], 1)
    a, b = shifted_waves(cols, order, coarse, device, devices)
    lift = jnp.concatenate([jnp.concatenate([a, -b], 1), jnp.concatenate([b, a], 1)], 0)

    cutoff = pupil_radius[0]
    shifted = (source_points - GRID // 2) * cutoff // shift_scale
    first = jnp.asarray(freq, jnp.int32)[None, None, :] + shifted[:, 0, None, None]
    second = jnp.asarray(order, jnp.int32)[None, :, None] + shifted[:, 1, None, None]
    passed = first * first + second * second <= cutoff * cutoff

    near, away = mask_field[:, :half], mask_field[:, half:]
    even = dot("xy,yq->xq", near + away, fold[0])
    odd = dot("xy,yq->xq", near - away, fold[1])
    part_c = jnp.concatenate([even[:, :kh], odd[:, :kh]], 1)
    part_s = jnp.concatenate([even[:, kh:], odd[:, kh:]], 1)
    spec = dot("xq,xk->qk", jnp.concatenate([part_c, part_s], 1), loc)
    band = jnp.concatenate(
        [spec[:K, :K] - spec[K:, K:], -(spec[:K, K:] + spec[K:, :K])], 0
    )
    band = lax.psum(band, "slab").reshape(2, K, K)

    kept = jnp.where(passed[:, None], band[None], 0.0).reshape(sources, 2 * K, K)
    wide = dot("aq,sqk->sak", lift, kept)
    both = dot("ak,kx->ax", wide.reshape(sources * 2 * cols, K), wave_x)
    both = both.reshape(sources, 2, cols, 2 * coarse)
    field_re = (both[:, 0, :, :coarse] - both[:, 1, :, coarse:]) * norming
    field_im = (both[:, 0, :, coarse:] + both[:, 1, :, :coarse]) * norming
    bright = field_re * field_re + field_im * field_im
    onehot = (source_groups[:, None] == jnp.arange(NG, dtype=jnp.int32)[None, :]).astype(jnp.float32)
    weights = jnp.exp(jnp.sum(onehot * group_logits[None, :], 1))
    total = jnp.sum(weights)
    share = weights / total
    image = jnp.sum(share[:, None, None] * bright, 0)

    tall = dot("cm,mx->cx", image, up)
    tall = lax.all_to_all(tall, "slab", 1, 0, tiled=True)
    intensity = dot("cx,cy->xy", tall, up)
    resist = jax.nn.sigmoid(steepness * (intensity - threshold))
    misfit = resist - target_print.astype(jnp.float32)
    slope = (2.0 * steepness) * misfit * resist * (1.0 - resist)
    squares = jnp.sum(misfit * misfit)
    down = dot("xy,cy->cx", slope, up)
    down = lax.all_to_all(down, "slab", 0, 1, tiled=True)
    pull = dot("cx,mx->cm", down, up)

    per_source = jnp.sum(bright * pull[None], (1, 2))
    sums = lax.psum(jnp.concatenate([per_source, squares[None]]), "slab")
    per_source, squares = sums[:-1], sums[-1]
    loss_value = (squares * norming).reshape(1)
    against = jnp.sum(share * per_source)
    source_pull = share * (per_source - against)
    group_grad = jnp.sum(onehot * source_pull[:, None], 0) * norming

    factor = (2.0 * norming) * share[:, None, None] * pull[None]
    back = jnp.stack([factor * field_re, factor * field_im], 1)
    low = dot("ax,kx->ak", back.reshape(sources * 2 * cols, coarse), wave_x[:, :coarse])
    lows = dot("ax,kx->ak", back.reshape(sources * 2 * cols, coarse), wave_x[:, coarse:])
    low = low.reshape(sources, 2, cols, K)
    lows = lows.reshape(sources, 2, cols, K)
    settle = jnp.concatenate([low[:, 0] + lows[:, 1], low[:, 1] - lows[:, 0]], 1)
    settle = dot("aq,sak->sqk", lift, settle).reshape(sources, 2, K, K)
    grad_band = jnp.sum(jnp.where(passed[:, None], settle, 0.0), 0)
    grad_band = lax.psum(grad_band.reshape(2 * K, K), "slab")

    loc_c2 = jnp.concatenate([loc_c, loc_s], 0)
    spread = dot("tk,qk->tq", loc_c2, grad_band)
    spread_re = spread[:rows, :K] - spread[rows:, K:]
    spread_im = spread[:rows, K:] + spread[rows:, :K]
    even = dot("xq,yq->xy", jnp.concatenate([spread_re[:, :kh], -spread_im[:, :kh]], 1), fold[0])
    odd = dot("xq,yq->xy", jnp.concatenate([spread_re[:, kh:], -spread_im[:, kh:]], 1), fold[1])
    mask_grad = jnp.concatenate([even + odd, even - odd], 1)
    return loss_value, mask_grad, group_grad


def solution(mesh):
    in_specs = (
        P(("clip", "slab"), None),
        P(("clip", "slab"), None),
        P("clip", None),
        P("clip"),
        P("clip"),
        P("clip"),
    )
    out_specs = (P("clip"), P(("clip", "slab"), None), P("clip"))
    return jax.shard_map(
        functools.partial(on_device, mesh.shape["slab"]),
        mesh=mesh, in_specs=in_specs, out_specs=out_specs, check_vma=False,
    )
```

time: 637 us -> 302 us (0.47); the launches traced: 628 us -> 301 us
  matrix products: 389 us -> 34.6 us
  blocking collectives: 32.7 us -> 58.7 us
  waiting for transfers between devices: 179 us -> 164 us
  other arithmetic: 5.88 us -> 15.6 us
  local copies, waits for them, and re-layouts: 3.85 us -> 11.1 us
    dot_general x30 -> x17, matrix products: 389 us -> 34.6 us  [dot(): jnp.einsum(form, left, right, precision=HIGH, preferred_element_type=jnp....]
    all_to_all x0 -> x2, blocking collectives: none -> 27.7 us  [the longest x1 15 us: on_device(): tall = lax.all_to_all(tall, 'slab', 1, 0, tiled=True)]
    psum x2, waiting for transfers between devices: 179 us -> 164 us  [the longest x1 86.3 us: on_device(): grad_band = lax.psum(grad_band.reshape(2 * K, K), 'slab')]
    concatenate x0 -> x4, other arithmetic: none -> 7.79 us  [the longest x1 5.18 us: on_device(): jnp.concatenate([jnp.roll(quarter, i * (n // 4), axis=1) for i in range(4...]
  transfers between devices with their start and end apart: 2 -> 2, of which waited for: 2 -> 2; matrix products, arithmetic and copies ran while one was open for 0% -> 5% of each run, Pallas kernels for 0% -> 0%
where the time goes in v1:
time: 302 us; the launch traced here: 301 us
  waiting for transfers between devices  164 us (54%)
  blocking collectives  58.7 us (19%)
  matrix products  34.6 us (11%)
  between operations  16.9 us (6%)
  other arithmetic  15.6 us (5%)
  local copies, waits for them, and re-layouts  11.1 us (4%)
    psum x1, waiting for transfers between devices, on_device(): grad_band = lax.psum(grad_band.reshape(2 * K, K), 'slab')  86.3 us
    psum x1, waiting for transfers between devices, on_device(): band = lax.psum(band, 'slab').reshape(2, K, K)  78.1 us
    dot_general x17, matrix products, dot(): jnp.einsum(form, left, right, precision=HIGH, preferred_element_type=jnp....  34.6 us
    psum x1, blocking collectives, on_device(): sums = lax.psum(jnp.concatenate([per_source, squares[None]]), 'slab')  31.1 us
    all_to_all x1, blocking collectives, on_device(): tall = lax.all_to_all(tall, 'slab', 1, 0, tiled=True)  15 us
    all_to_all x1, blocking collectives, on_device(): down = lax.all_to_all(down, 'slab', 0, 1, tiled=True)  12.7 us
  transfers between devices with their start and end apart: 2, of which 2 were waited for; matrix products, arithmetic and copies ran while one was open for 5% of the time, Pallas kernels for 0%

profile of v1, /device:TPU:0, one launch (start us, length us, event | category | flops | bytes accessed | tf_op | source)
XLA Modules:
  0.0 301.4 jit_solution(10782398670884139103)
XLA Ops:
  7.2 2.0 fusion.31
  9.3 2.0 fusion.29
  11.3 0.8 constant_dynamic-slice_fusion
  12.1 1.0 multiply_subtract_fusion
  13.1 0.6 fusion.41
  13.8 0.9 pad_maximum_fusion.4
  14.8 0.9 fusion.73
  15.6 0.9 fusion.75
  16.5 0.1 fusion.74
  17.2 0.1 select_reduce_fusion.1
  17.3 0.6 exponential_reduce_fusion
  18.1 0.9 add_compare_fusion
  18.9 5.2 %maximum_maximum_fusion = f32[512,2048]{0,1:T(8,128)} fusion(f32[128,512]{0,1:T(8,128)} %get-tuple-element.12, f32[128,1536]{0,1:T(8,128)S(1)} %get-tuple-element.14, f32[128,1024]{0,1:T(8,128)} %get-tuple-element.16, f32[128,1024]{0,1:T(8,128)S(1)} %get-tuple-element.15, f32[128,1536]{0,1:T(8,128)S(1)} %get-tuple-element.13, ...), kind=kLoop, calls=%fused_computation.4 | loop fusion | flops 6291456 | bytes 8388608 | tf_op jit(solution)/shard_map/concatenate | solution.py:68
  24.1 0.7 broadcast_multiply_fusion.1
  24.8 1.0 broadcast_in_dim.28
  25.8 4.3 %copy.46 = pred[16,512,256]{1,2,0:T(32,128)(4,1)S(1)} copy(pred[16,512,256]{2,1,0:T(32,128)(4,1)S(1)} %bitcast.90) | data formatting | bytes 4194304 | tf_op jit(solution)/shard_map/jit(_where)/broadcast_in_dim | solution.py:93
  30.2 78.1 %all-reduce.3.cloned.1.call-done = f32[512,256]{1,0:T(8,128)} async-done(((f32[512,256]{1,0:T(8,128)}), f32[512,256]{1,0:T(8,128)}) %all-reduce.3.cloned.1.call-update) | async-done | bytes 524304 | tf_op jit(solution)/shard_map/psum | solution.py:91
  108.3 2.0 copy.45
  110.3 5.4 %fusion.1 = f32[16,256,64]{1,2,0:T(8,128)S(1)} fusion(pred[16,512,256]{1,2,0:T(32,128)(4,1)S(1)} %copy.46, f32[512,256]{0,1:T(8,128)} %copy.45, f32[32,256]{1,0:T(8,128)S(1)} %get-tuple-element.27, f32[32,256]{1,0:T(8,128)S(1)} %get-tuple-element.26, f32[32,256]{1,0:T(8,128)S(1)} %get-tuple-element.25), kind=kOutput, calls=%fused_computation.2 | convolution fusion | flops 807501824 | bytes 3768320 | tf_op jit(solution)/shard_map/aq,sqk->sak/dot_general | solution.py:21
  115.7 1.9 fusion.78
  117.6 0.5 fusion.17
  118.1 2.0 fusion.60
  120.2 15.0 %all_to_all.35 = f32[32,16,128]{2,0,1:T(8,128)S(1)} all-to-all(f32[32,16,128]{2,0,1:T(8,128)S(1)} %fusion.60), channel_id=1, replica_groups=mesh['clip'=2,'slab'=16] {'slab'}, dimensions={1} | all-to-all | bytes 524288 | tf_op jit(solution)/shard_map/all_to_all | solution.py:107
  135.1 2.8 multiply_reduce_fusion
  137.9 3.5 %fusion.19 = f32[512,128]{1,0:T(8,128)S(1)} fusion(f32[512,2048]{0,1:T(8,128)S(1)} %copy-done, f32[128,2048]{1,0:T(8,128)S(1)} %get-tuple-element.35, s32[128,2048]{1,0:T(8,128)S(1)} %copy-done.2), kind=kOutput, calls=%fused_computation.34 | convolution fusion | flops 806879232 | bytes 6553600 | tf_op jit(solution)/shard_map/xy,cy->cx/dot_general | solution.py:21
  141.4 12.7 %all_to_all.36 = f32[16,32,128]{2,1,0:T(8,128)S(1)} all-to-all(f32[16,32,128]{2,1,0:T(8,128)S(1)} %bitcast.91), channel_id=1, replica_groups=mesh['clip'=2,'slab'=16] {'slab'}, dimensions={0} | all-to-all | bytes 524288 | tf_op jit(solution)/shard_map/all_to_all | solution.py:114
  154.1 1.5 fusion.37
  155.5 0.4 fusion.18
  156.0 0.6 multiply_multiply_fusion.1
  156.6 0.4 copy-done.6
  157.0 1.0 fusion.10
  158.1 1.0 fusion.11
  159.1 0.7 pad_maximum_fusion.5
  159.9 0.9 fusion.26
  160.8 31.1 %psum.22 = f32[17]{0:T(128)S(1)} all-reduce(f32[17]{0:T(128)S(1)} %pad_maximum_fusion.5), channel_id=1, replica_groups=mesh['clip'=2,'slab'=16] {'slab'}, use_global_device_ids=true, to_apply=%region_6.7 | all-reduce | flops 17 | bytes 136 | tf_op jit(solution)/shard_map/psum | solution.py:118
  191.8 0.6 multiply_reduce_fusion.1
  192.4 0.6 subtract_multiply_fusion
  193.1 5.9 %fusion = f32[512,256]{0,1:T(8,128)} fusion(pred[16,512,256]{1,2,0:T(32,128)(4,1)S(1)} %copy.46, f32[16,32,256]{2,1,0:T(8,128)S(1)} %fusion.24, f32[16,32,256]{2,1,0:T(8,128)} %fusion.26, f32[32,256]{1,0:T(8,128)S(1)} %get-tuple-element.27, f32[32,256]{1,0:T(8,128)S(1)} %get-tuple-element.26, f32[32,256]{1,0:T(8,128)S(1)} %get-tuple-element.25), kind=kOutput, calls=%fused_computation.1 | convolution fusion | flops 809730048 | bytes 3768320 | tf_op jit(solution)/shard_map/aq,sak->sqk/dot_general | solution.py:21
  199.0 0.1 select_reduce_fusion
  199.2 0.6 slice.161
  200.4 0.5 broadcast_multiply_fusion
  200.9 86.3 %all-reduce.5.cloned.1.call-done = f32[512,256]{0,1:T(8,128)} async-done(((f32[512,256]{0,1:T(8,128)}), f32[512,256]{0,1:T(8,128)}) %all-reduce.5.cloned.1.call-update) | async-done | bytes 524304 | tf_op jit(solution)/shard_map/psum | solution.py:134
  287.2 1.4 fusion.52
  288.7 1.4 fusion.56
  290.1 1.4 fusion.58
  291.5 0.4 convolution_add_fusion.1
  291.9 0.4 fusion.72
  292.4 1.0 pad_maximum_fusion.3
  (41 shorter events, 0.5 us)
Async XLA Ops:
  7.2 101.1 %all-reduce.3.cloned.1.call-start = ((), (), s32[]{:S(2)}) async-start(), calls=%async_computation.2 | async-start | bytes 1048576 | tf_op jit(solution)/shard_map/psum | solution.py:91
  7.2 7.5 %copy-start.1 = (f32[128,2048]{0,1:T(8,128)S(1)}, f32[128,2048]{0,1:T(8,128)}, u32[]{:S(2)}) copy-start(f32[128,2048]{0,1:T(8,128)} %constant.68.clone) | copy-start | bytes 3145732
  13.8 3.5 %copy-start.13 = (f32[8]{0:T(128)S(1)}, f32[8]{0:T(128)}, u32[]{:S(2)}) copy-start(f32[8]{0:T(128)} %param.22) | copy-start | bytes 100
  13.8 3.5 %copy-start.14 = (s32[16]{0:T(128)S(1)}, s32[16]{0:T(128)}, u32[]{:S(2)}) copy-start(s32[16]{0:T(128)} %param.21) | copy-start | bytes 196
  13.8 4.2 %copy-start.12 = (s32[16,2]{0,1:T(2,128)S(1)}, s32[16,2]{0,1:T(2,128)}, u32[]{:S(2)}) copy-start(s32[16,2]{0,1:T(2,128)} %param.20) | copy-start | bytes 388
  13.8 4.2 %copy-start.10 = (s32[256]{0:T(256)S(1)}, s32[256]{0:T(256)}, u32[]{:S(2)}) copy-start(s32[256]{0:T(256)} %constant.77.clone) | copy-start | bytes 3076
  13.8 4.2 %copy-start.11 = (s32[256]{0:T(256)S(1)}, s32[256]{0:T(256)}, u32[]{:S(2)}) copy-start(s32[256]{0:T(256)} %constant.76.clone) | copy-start | bytes 3076
  14.7 272.5 %all-reduce.5.cloned.1.call-start = ((), (), s32[]{:S(2)}) async-start(), calls=%async_computation.3 | async-start | bytes 1048576 | tf_op jit(solution)/shard_map/psum | solution.py:134
  24.1 6.0 %copy-start.8 = (f32[32,256]{1,0:T(8,128)S(1)}, f32[32,256]{1,0:T(8,128)}, u32[]{:S(2)}) copy-start(f32[32,256]{1,0:T(8,128)} %constant.75.clone) | copy-start | bytes 98308
  24.1 6.0 %copy-start.9 = (f32[32,256]{1,0:T(8,128)S(1)}, f32[32,256]{1,0:T(8,128)}, u32[]{:S(2)}) copy-start(f32[32,256]{1,0:T(8,128)} %constant.74.clone) | copy-start | bytes 98308
  25.8 89.9 %copy-start.3 = (f32[256,1024,1,1]{1,0,3,2:T(8,128)S(1)}, f32[256,1024,1,1]{1,0,3,2:T(8,128)}, u32[]{:S(2)}) copy-start(f32[256,1024,1,1]{1,0,3,2:T(8,128)} %constant.85) | copy-start | bytes 3145732
  115.7 2.4 copy-start
  117.6 17.6 %copy-start.2 = (s32[128,2048]{1,0:T(8,128)S(1)}, s32[128,2048]{1,0:T(8,128)}, u32[]{:S(2)}) copy-start(s32[128,2048]{1,0:T(8,128)} %param.19) | copy-start | bytes 3145732
  156.0 1.0 copy-start.6
  156.0 2.1 copy-start.5
  193.1 98.4 %copy-start.4 = (f32[1024,128]{1,0:T(8,128)S(1)}, f32[1024,128]{1,0:T(8,128)}, u32[]{:S(2)}) copy-start(f32[1024,128]{1,0:T(8,128)} %constant.84) | copy-start | bytes 1572868
  199.0 92.9 %copy-start.7 = (f32[1024,128]{1,0:T(8,128)S(1)}, f32[1024,128]{1,0:T(8,128)}, u32[]{:S(2)}) copy-start(f32[1024,128]{1,0:T(8,128)} %constant.82) | copy-start | bytes 1572868
Sparse Core Ops, SparseCore 0:
  14.8 93.4 all-reduce.2
  199.2 87.9 all-reduce.4

commit v2 on v1

--- a/solution.py
+++ b/solution.py
@@ -41,6 +41,14 @@
     return turned((far[0], far[1]), (jnp.asarray(near[0]), jnp.asarray(near[1])))
 
 
+def exchange(blocks):
+    return lax.all_to_all(blocks, "slab", 0, 0)
+
+
+def gather(block, devices):
+    return lax.all_gather(block, "slab", tiled=True)
+
+
 def on_device(devices, mask_field, target_print, source_points, source_groups, group_logits, pupil_radius):
     rows, n = mask_field.shape
     sources = source_points.shape[0]
@@ -59,13 +67,12 @@
         jnp.asarray(np.concatenate([t[:, p * kh : (p + 1) * kh] for t in (cos_y, sin_y)], 1), jnp.float32)
         for p in (0, 1)
     ]
-    lag = np.mod(np.arange(n)[None, :] - step * np.arange(coarse // 4)[:, None], n)
+    lag = np.mod(np.arange(n)[None, :] - step * np.arange(coarse)[:, None], n)
     kernel = np.zeros(n)
     for f in range(1, K):
         kernel += 2.0 * np.cos(2.0 * math.pi * np.mod(f * np.arange(n), n) / n)
     kernel = (kernel + 1.0) / coarse
-    quarter = lax.optimization_barrier(jnp.asarray(kernel[lag], jnp.float32))
-    up = jnp.concatenate([jnp.roll(quarter, i * (n // 4), axis=1) for i in range(4)], 0)
+    up = jnp.asarray(kernel[lag], jnp.float32)
     cos_c, sin_c = waves(freq, np.arange(coarse), coarse)
     wave_x = jnp.asarray(np.concatenate([cos_c, sin_c], 1), jnp.float32)
     loc_c, loc_s = shifted_waves(rows, freq, n, device, devices)
@@ -76,7 +83,7 @@
     cutoff = pupil_radius[0]
     shifted = (source_points - GRID // 2) * cutoff // shift_scale
     first = jnp.asarray(freq, jnp.int32)[None, None, :] + shifted[:, 0, None, None]
-    second = jnp.asarray(order, jnp.int32)[None, :, None] + shifted[:, 1, None, None]
+    second = jnp.asarray(np.tile(order, 2), jnp.int32)[None, :, None] + shifted[:, 1, None, None]
     passed = first * first + second * second <= cutoff * cutoff
 
     near, away = mask_field[:, :half], mask_field[:, half:]
@@ -88,9 +95,10 @@
     band = jnp.concatenate(
         [spec[:K, :K] - spec[K:, K:], -(spec[:K, K:] + spec[K:, :K])], 0
     )
-    band = lax.psum(band, "slab").reshape(2, K, K)
+    band = jnp.sum(exchange(band.reshape(devices, 2 * K // devices, K)), 0)
+    band = gather(band, devices)
 
-    kept = jnp.where(passed[:, None], band[None], 0.0).reshape(sources, 2 * K, K)
+    kept = jnp.where(passed, band[None], 0.0)
     wide = dot("aq,sqk->sak", lift, kept)
     both = dot("ak,kx->ax", wide.reshape(sources * 2 * cols, K), wave_x)
     both = both.reshape(sources, 2, cols, 2 * coarse)
@@ -115,13 +123,7 @@
     pull = dot("cx,mx->cm", down, up)
 
     per_source = jnp.sum(bright * pull[None], (1, 2))
-    sums = lax.psum(jnp.concatenate([per_source, squares[None]]), "slab")
-    per_source, squares = sums[:-1], sums[-1]
-    loss_value = (squares * norming).reshape(1)
-    against = jnp.sum(share * per_source)
-    source_pull = share * (per_source - against)
-    group_grad = jnp.sum(onehot * source_pull[:, None], 0) * norming
-
+    sums = jnp.concatenate([per_source, squares[None]])
     factor = (2.0 * norming) * share[:, None, None] * pull[None]
     back = jnp.stack([factor * field_re, factor * field_im], 1)
     low = dot("ax,kx->ak", back.reshape(sources * 2 * cols, coarse), wave_x[:, :coarse])
@@ -129,9 +131,19 @@
     low = low.reshape(sources, 2, cols, K)
     lows = lows.reshape(sources, 2, cols, K)
     settle = jnp.concatenate([low[:, 0] + lows[:, 1], low[:, 1] - lows[:, 0]], 1)
-    settle = dot("aq,sak->sqk", lift, settle).reshape(sources, 2, K, K)
-    grad_band = jnp.sum(jnp.where(passed[:, None], settle, 0.0), 0)
-    grad_band = lax.psum(grad_band.reshape(2 * K, K), "slab")
+    settle = dot("aq,sak->sqk", lift, settle)
+    grad_band = jnp.sum(jnp.where(passed, settle, 0.0), 0).reshape(devices, 2 * K // devices, K)
+    extra = jnp.pad(sums[None, :], ((0, 7), (0, K - sources - 1)))
+    extra = jnp.broadcast_to(extra[None], (devices, 8, K))
+    grad_band = jnp.sum(exchange(jnp.concatenate([grad_band, extra], 1)), 0)
+    sums = grad_band[-8, : sources + 1]
+    grad_band = gather(grad_band[:-8], devices)
+    per_source, squares = sums[:-1], sums[-1]
+    loss_value = (squares * norming).reshape(1)
+    against = jnp.sum(share * per_source)
+    source_pull = share * (per_source - against)
+    group_grad = jnp.sum(onehot * source_pull[:, None], 0) * norming
+
 
     loc_c2 = jnp.concatenate([loc_c, loc_s], 0)
     spread = dot("tk,qk->tq", loc_c2, grad_band)

time: 302 us -> 151 us (0.50)
  waiting for transfers between devices: 164 us -> 12 us
  blocking collectives: 58.7 us -> 88.5 us
  between operations: 16.9 us -> 3.55 us
  local copies, waits for them, and re-layouts: 11.1 us -> 2.46 us
  starting transfers between devices: 0.08 us -> 7.41 us
  matrix products: 34.6 us -> 27.8 us
  other arithmetic: 15.6 us -> 8.98 us
    psum x2 -> x0, waiting for transfers between devices: 164 us -> none  [the longest x1 86.3 us: on_device(): grad_band = lax.psum(grad_band.reshape(2 * K, K), 'slab')]
    all_gather x0 -> x2, blocking collectives: none -> 41.7 us  [gather(): return lax.all_gather(block, 'slab', tiled=True)]
    psum x1 -> x0, blocking collectives: 31.1 us -> none  [on_device(): sums = lax.psum(jnp.concatenate([per_source, squares[None]]), 'slab')]
    all_to_all x0 -> x1, blocking collectives: none -> 21.1 us  [exchange(): return lax.all_to_all(blocks, 'slab', 0, 0)]
    all_to_all x0 -> x1, waiting for transfers between devices: none -> 12 us  [exchange(): return lax.all_to_all(blocks, 'slab', 0, 0)]
    all_to_all x0 -> x1, starting transfers between devices: none -> 7.41 us  [exchange(): return lax.all_to_all(blocks, 'slab', 0, 0)]
    dot_general x17, matrix products: 34.6 us -> 27.8 us  [dot(): jnp.einsum(form, left, right, precision=HIGH, preferred_element_type=jnp....]
    concatenate x2 -> x1, other arithmetic: 5.9 us -> 0.05 us  [on_device(): grad_band = jnp.sum(exchange(jnp.concatenate([grad_band, extra], 1)), 0)]
  transfers between devices with their start and end apart: 2 -> 1, of which waited for: 2 -> 1; matrix products, arithmetic and copies ran while one was open for 5% -> 1% of each run, Pallas kernels for 0% -> 0%
where the time goes in v2:
time: 151 us
  blocking collectives  88.5 us (59%)
  matrix products  27.8 us (18%)
  waiting for transfers between devices  12 us (8%)
  other arithmetic  8.98 us (6%)
  starting transfers between devices  7.41 us (5%)
  between operations  3.55 us (2%)
  local copies, waits for them, and re-layouts  2.46 us (2%)
    all_gather x2, blocking collectives, gather(): return lax.all_gather(block, 'slab', tiled=True)  41.7 us
    dot_general x17, matrix products, dot(): jnp.einsum(form, left, right, precision=HIGH, preferred_element_type=jnp....  27.8 us
    all_to_all x1, blocking collectives, exchange(): return lax.all_to_all(blocks, 'slab', 0, 0)  21.1 us
    all_to_all x1, blocking collectives, on_device(): tall = lax.all_to_all(tall, 'slab', 1, 0, tiled=True)  12.9 us
    all_to_all x1, blocking collectives, on_device(): down = lax.all_to_all(down, 'slab', 0, 1, tiled=True)  12.8 us
    all_to_all x1, waiting for transfers between devices, exchange(): return lax.all_to_all(blocks, 'slab', 0, 0)  12 us
    all_to_all x1, starting transfers between devices, exchange(): return lax.all_to_all(blocks, 'slab', 0, 0)  7.41 us
  transfers between devices with their start and end apart: 1, of which 1 were waited for; matrix products, arithmetic and copies ran while one was open for 1% of the time, Pallas kernels for 0%

profile of v2, /device:TPU:0, one launch (start us, length us, event | category | flops | bytes accessed | tf_op | source)
XLA Modules:
  0.0 150.6 jit_solution(6322485100976151592)
XLA Ops:
  0.6 2.0 %fusion.29 = f32[128,256]{1,0:T(8,128)S(1)} fusion(f32[1024,256]{1,0:T(8,128)} %constant.67.clone, f32[128,2048]{1,0:T(8,128)} %param.18), kind=kOutput, calls=%fused_computation.51 | convolution fusion | flops 201457664 | bytes 2228224 | tf_op jit(solution)/shard_map/xy,yq->xq/dot_general | solution.py:21
  2.7 2.0 %fusion.27 = f32[128,256]{1,0:T(8,128)S(1)} fusion(f32[1024,256]{1,0:T(8,128)} %constant.68.clone, f32[128,2048]{1,0:T(8,128)} %param.18), kind=kOutput, calls=%fused_computation.49 | convolution fusion | flops 201457664 | bytes 2228224 | tf_op jit(solution)/shard_map/xy,yq->xq/dot_general | solution.py:21
  4.7 0.8 constant_dynamic-slice_fusion
  5.5 1.0 multiply_subtract_fusion
  6.5 0.6 fusion.37
  7.2 0.8 pad_maximum_fusion.5
  8.0 7.4 %all-to-all-start = ((f32[16,32,256]{2,1,0:T(8,128)}), f32[16,32,256]{2,1,0:T(8,128)S(1)}, u32[]{:S(2)}, u32[]{:S(2)}) async-start(f32[16,32,256]{2,1,0:T(8,128)} %bitcast.5), calls=%async_computation | async-start | bytes 1048576 | tf_op jit(solution)/shard_map/all_to_all | solution.py:45
  16.1 0.1 select_reduce_fusion.1
  16.2 0.6 exponential_reduce_fusion
  16.8 0.7 broadcast_multiply_fusion.1
  17.5 0.1 add_multiply_fusion.1
  17.6 0.1 add_multiply_fusion
  17.7 12.0 %all-to-all-done = f32[16,32,256]{2,1,0:T(8,128)S(1)} async-done(((f32[16,32,256]{2,1,0:T(8,128)}), f32[16,32,256]{2,1,0:T(8,128)S(1)}, u32[]{:S(2)}, u32[]{:S(2)}) %all-to-all-start) | async-done | bytes 524320 | tf_op jit(solution)/shard_map/all_to_all | solution.py:45
  29.7 21.3 %all_gather.6 = f32[512,256]{1,0:T(8,128)S(1)} all-gather(f32[32,256]{1,0:T(8,128)S(1)} %reduce_sum.92), channel_id=1, replica_groups=mesh['clip'=2,'slab'=16] {'slab'}, dimensions={0}, use_global_device_ids=true | all-gather | bytes 557056 | tf_op jit(solution)/shard_map/all_gather | solution.py:49
  51.1 0.2 copy.43
  51.3 4.5 %fusion.1 = f32[16,256,64]{1,2,0:T(8,128)S(1)} fusion(f32[512,256]{0,1:T(8,128)S(1)} %copy.43, s32[]{:T(128)S(6)} %mul.218, s32[16,512]{1,0:T(8,128)S(1)} %add_multiply_fusion, s32[16,256]{1,0:T(8,128)S(1)} %add_multiply_fusion.1, f32[32,256]{1,0:T(8,128)S(1)} %get-tuple-element.21, f32[32,256]{1,0:T(8,128)S(1)} %get-tuple-element.20, ...), kind=kOutput, calls=%fused_computation.2 | convolution fusion | flops 811696128 | bytes 1720324 | tf_op jit(solution)/shard_map/aq,sqk->sak/dot_general | solution.py:21
  55.7 1.9 %fusion.72 = f32[16,2,32,1024]{3,2,1,0:T(8,128)S(1)} fusion(f32[16,2,32,256]{3,2,1,0:T(8,128)S(1)} %bitcast.96, f32[256,1024,1,1]{1,0,3,2:T(8,128)S(1)} %copy-done.4), kind=kOutput, calls=%fused_computation.126 | convolution fusion | flops 1610612736 | bytes 6291456 | tf_op jit(solution)/shard_map/ak,kx->ax/dot_general | solution.py:21
  57.6 0.5 fusion.20
  58.2 2.0 %fusion.57 = f32[32,16,128]{2,0,1:T(8,128)S(1)} fusion(f32[16,128,512]{2,1,0:T(8,128)S(1)} %copy-done.1, f32[32,512]{1,0:T(8,128)S(1)} %fusion.20), kind=kOutput, calls=%fused_computation.89 | convolution fusion | flops 201326592 | bytes 4521984 | tf_op jit(solution)/shard_map/cm,mx->cx/dot_general | solution.py:21
  60.2 12.9 %all_to_all.45 = f32[32,16,128]{2,0,1:T(8,128)S(1)} all-to-all(f32[32,16,128]{2,0,1:T(8,128)S(1)} %fusion.57), channel_id=1, replica_groups=mesh['clip'=2,'slab'=16] {'slab'}, dimensions={1} | all-to-all | bytes 524288 | tf_op jit(solution)/shard_map/all_to_all | solution.py:115
  73.1 0.2 copy.45
  73.3 2.4 %multiply_reduce_fusion = (f32[]{:T(128)}, f32[128,2048]{1,0:T(8,128)S(1)}) fusion(s32[128,2048]{1,0:T(8,128)S(1)} %copy-done.2, f32[512,128]{1,0:T(8,128)S(1)} %bitcast.97, f32[512,2048]{1,0:T(8,128)S(1)} %copy-done.3), kind=kOutput, calls=%fused_computation.35 | convolution fusion | flops 807665664 | bytes 6553604 | tf_op jit(solution)/shard_map/cx,cy->xy/dot_general | solution.py:21
  75.7 1.9 %fusion.22 = f32[512,128]{1,0:T(8,128)S(1)} fusion(f32[512,2048]{1,0:T(8,128)S(1)} %copy-done, f32[128,2048]{1,0:T(8,128)S(1)} %get-tuple-element.29, s32[128,2048]{1,0:T(8,128)S(1)} %copy-done.2), kind=kOutput, calls=%fused_computation.39 | convolution fusion | flops 806879232 | bytes 6553600 | tf_op jit(solution)/shard_map/xy,cy->cx/dot_general | solution.py:21
  77.6 12.8 %all_to_all.46 = f32[16,32,128]{2,1,0:T(8,128)S(1)} all-to-all(f32[16,32,128]{2,1,0:T(8,128)S(1)} %bitcast.95), channel_id=1, replica_groups=mesh['clip'=2,'slab'=16] {'slab'}, dimensions={0} | all-to-all | bytes 524288 | tf_op jit(solution)/shard_map/all_to_all | solution.py:122
  90.3 2.0 %fusion.52 = f32[32,512]{1,0:T(8,128)S(1)} fusion(f32[512,2048]{1,0:T(8,128)S(1)} %copy-done, f32[16,32,128]{2,1,0:T(8,128)S(1)} %all_to_all.46), kind=kOutput, calls=%fused_computation.77 | convolution fusion | flops 201326592 | bytes 4521984 | tf_op jit(solution)/shard_map/cx,mx->cm/dot_general | solution.py:21
  92.4 0.4 fusion.21
  92.8 0.6 multiply_multiply_fusion.1
  93.4 0.4 copy-done.7
  93.8 1.0 fusion.13
  94.9 1.0 fusion.14
  95.9 0.1 fusion.23
  96.0 0.1 fusion.25
  96.1 0.7 maximum_bitcast_fusion.3
  96.8 4.5 %fusion = f32[512,256]{0,1:T(8,128)S(1)} fusion(s32[]{:T(128)S(6)} %mul.218, s32[16,512]{1,0:T(8,128)S(1)} %add_multiply_fusion, s32[16,256]{1,0:T(8,128)S(1)} %add_multiply_fusion.1, f32[16,32,256]{2,1,0:T(8,128)S(1)} %fusion.23, f32[16,32,256]{2,1,0:T(8,128)S(1)} %fusion.25, f32[32,256]{1,0:T(8,128)S(1)} %get-tuple-element.21, ...), kind=kOutput, calls=%fused_computation.1 | convolution fusion | flops 813924352 | bytes 1720324 | tf_op jit(solution)/shard_map/aq,sak->sqk/dot_general | solution.py:21
  101.4 0.2 copy.49
  101.7 21.1 %all_to_all.47 = f32[16,40,256]{2,1,0:T(8,128)S(1)} all-to-all(f32[16,40,256]{2,1,0:T(8,128)S(1)} %pad_maximum_fusion.4), channel_id=1, replica_groups=mesh['clip'=2,'slab'=16] {'slab'}, dimensions={0} | all-to-all | bytes 1310720 | tf_op jit(solution)/shard_map/all_to_all | solution.py:45
  122.8 0.6 multiply_reduce_fusion.1
  123.4 0.6 slice.179
  124.0 0.6 subtract_multiply_fusion.2
  124.7 0.1 select_reduce_fusion
  124.8 0.5 broadcast_multiply_fusion
  125.3 20.4 %all_gather.7 = f32[512,256]{1,0:T(8,128)S(1)} all-gather(f32[32,256]{1,0:T(8,128)S(1)} %slice.180), channel_id=1, replica_groups=mesh['clip'=2,'slab'=16] {'slab'}, dimensions={0}, use_global_device_ids=true | all-gather | bytes 557056 | tf_op jit(solution)/shard_map/all_gather | solution.py:49
  145.7 0.4 fusion.48
  146.2 0.4 fusion.53
  146.6 0.4 fusion.55
  147.6 0.4 convolution_add_fusion.1
  148.0 0.4 fusion.69
  148.5 1.0 pad_maximum_fusion.3
  (47 shorter events, 0.4 us)
Async XLA Ops:
  2.6 13.5 %copy-start.16 = (f32[8]{0:T(128)S(1)}, f32[8]{0:T(128)}, u32[]{:S(2)}) copy-start(f32[8]{0:T(128)} %param.22) | copy-start | bytes 100
  2.6 13.5 %copy-start.17 = (s32[16]{0:T(128)S(1)}, s32[16]{0:T(128)}, u32[]{:S(2)}) copy-start(s32[16]{0:T(128)} %param.21) | copy-start | bytes 196
  2.6 14.2 %copy-start.15 = (s32[16,2]{0,1:T(2,128)S(1)}, s32[16,2]{0,1:T(2,128)}, u32[]{:S(2)}) copy-start(s32[16,2]{0,1:T(2,128)} %param.20) | copy-start | bytes 388
  2.6 14.8 %copy-start.14 = (s32[256]{0:T(256)S(1)}, s32[256]{0:T(256)}, u32[]{:S(2)}) copy-start(s32[256]{0:T(256)} %constant.77.clone) | copy-start | bytes 3076
  2.7 14.9 %copy-start.13 = (s32[512]{0:T(512)S(1)}, s32[512]{0:T(512)}, u32[]{:S(2)}) copy-start(s32[512]{0:T(512)} %constant.78.clone) | copy-start | bytes 6148
  2.7 15.0 %copy-start.11 = (f32[32,256]{1,0:T(8,128)S(1)}, f32[32,256]{1,0:T(8,128)}, u32[]{:S(2)}) copy-start(f32[32,256]{1,0:T(8,128)} %constant.76.clone) | copy-start | bytes 98308
  2.7 15.0 %copy-start.12 = (f32[32,256]{1,0:T(8,128)S(1)}, f32[32,256]{1,0:T(8,128)}, u32[]{:S(2)}) copy-start(f32[32,256]{1,0:T(8,128)} %constant.75.clone) | copy-start | bytes 98308
  8.0 21.7 %all-to-all-start = ((f32[16,32,256]{2,1,0:T(8,128)}), f32[16,32,256]{2,1,0:T(8,128)S(1)}, u32[]{:S(2)}, u32[]{:S(2)}) async-start(f32[16,32,256]{2,1,0:T(8,128)} %bitcast.5), calls=%async_computation | async-start | bytes 1048576 | tf_op jit(solution)/shard_map/all_to_all | solution.py:45
  51.3 4.5 %copy-start.4 = (f32[256,1024,1,1]{1,0,3,2:T(8,128)S(1)}, f32[256,1024,1,1]{1,0,3,2:T(8,128)}, u32[]{:S(2)}) copy-start(f32[256,1024,1,1]{1,0,3,2:T(8,128)} %constant.93) | copy-start | bytes 3145732
  55.7 2.5 %copy-start.1 = (f32[16,128,512]{2,1,0:T(8,128)S(1)}, f32[16,128,512]{2,1,0:T(8,128)}, u32[]{:S(2)}) copy-start(f32[16,128,512]{2,1,0:T(8,128)} %constant.83) | copy-start | bytes 12582916
  57.6 15.6 %copy-start.2 = (s32[128,2048]{1,0:T(8,128)S(1)}, s32[128,2048]{1,0:T(8,128)}, u32[]{:S(2)}) copy-start(s32[128,2048]{1,0:T(8,128)} %param.19) | copy-start | bytes 3145732
  57.6 15.6 %copy-start.3 = (f32[512,2048]{1,0:T(8,128)S(1)}, f32[512,2048]{1,0:T(8,128)}, u32[]{:S(2)}) copy-start(f32[512,2048]{1,0:T(8,128)} %constant.86) | copy-start | bytes 12582916
  60.2 15.5 %copy-start = (f32[512,2048]{1,0:T(8,128)S(1)}, f32[512,2048]{1,0:T(8,128)}, u32[]{:S(2)}) copy-start(f32[512,2048]{1,0:T(8,128)} %constant.69.clone) | copy-start | bytes 12582916
  92.8 1.0 copy-start.7
  92.8 2.1 %copy-start.6 = (f32[256,512,1,1]{1,0,3,2:T(8,128)S(1)}, f32[256,512,1,1]{1,0,3,2:T(8,128)}, u32[]{:S(2)}) copy-start(f32[256,512,1,1]{1,0,3,2:T(8,128)} %constant.94) | copy-start | bytes 1572868
  101.4 44.8 %copy-start.9 = (f32[1024,128]{1,0:T(8,128)S(1)}, f32[1024,128]{1,0:T(8,128)}, u32[]{:S(2)}) copy-start(f32[1024,128]{1,0:T(8,128)} %constant.91) | copy-start | bytes 1572868
  101.4 45.2 %copy-start.8 = (f32[1024,128]{1,0:T(8,128)S(1)}, f32[1024,128]{1,0:T(8,128)}, u32[]{:S(2)}) copy-start(f32[1024,128]{1,0:T(8,128)} %constant.89) | copy-start | bytes 1572868
  101.6 46.0 %copy-start.5 = (f32[1024,128]{1,0:T(8,128)S(1)}, f32[1024,128]{1,0:T(8,128)}, u32[]{:S(2)}) copy-start(f32[1024,128]{1,0:T(8,128)} %constant.92) | copy-start | bytes 1572868
  101.7 46.4 %copy-start.10 = (f32[1024,128]{1,0:T(8,128)S(1)}, f32[1024,128]{1,0:T(8,128)}, u32[]{:S(2)}) copy-start(f32[1024,128]{1,0:T(8,128)} %constant.90) | copy-start | bytes 1572868

commit v3 on v2

--- a/solution.py
+++ b/solution.py
@@ -5,6 +5,8 @@
 import jax.numpy as jnp
 import numpy as np
 from jax import lax
+from jax.experimental import pallas as pl
+from jax.experimental.pallas import tpu as pltpu
 from jax.sharding import PartitionSpec as P
 
 K = 256
@@ -41,12 +43,74 @@
     return turned((far[0], far[1]), (jnp.asarray(near[0]), jnp.asarray(near[1])))
 
 
-def exchange(blocks):
-    return lax.all_to_all(blocks, "slab", 0, 0)
-
-
-def gather(block, devices):
-    return lax.all_gather(block, "slab", tiled=True)
+def greet(me, devices):
+    barrier = pltpu.get_barrier_semaphore()
+
+    def signal(o, carry):
+        pl.semaphore_signal(
+            barrier, inc=1, device_id={"slab": lax.rem(me + o, devices)},
+            device_id_type=pl.DeviceIdType.MESH,
+        )
+        return carry
+
+    lax.fori_loop(1, devices, signal, 0)
+    pl.semaphore_wait(barrier, devices - 1)
+
+
+def spread_kernel(devices, whole, in_ref, out_ref, send_sem, recv_sem, own_sem):
+    me = lax.axis_index("slab")
+    mine = in_ref if whole else in_ref.at[me]
+    own = pltpu.make_async_copy(mine, out_ref.at[me], own_sem)
+    own.start()
+    greet(me, devices)
+
+    def transfer(o):
+        peer = lax.rem(me + o, devices)
+        return pltpu.make_async_remote_copy(
+            src_ref=in_ref if whole else in_ref.at[peer],
+            dst_ref=out_ref.at[me],
+            send_sem=send_sem.at[o],
+            recv_sem=recv_sem.at[o],
+            device_id={"slab": peer},
+            device_id_type=pl.DeviceIdType.MESH,
+        )
+
+    def start(o, carry):
+        transfer(o).start()
+        return carry
+
+    def finish(o, carry):
+        transfer(o).wait()
+        return carry
+
+    lax.fori_loop(1, devices, start, 0)
+    own.wait()
+    lax.fori_loop(1, devices, finish, 0)
+
+
+def spread(block, devices, whole, number):
+    shape = block.shape if not whole else (devices,) + block.shape
+    return pl.pallas_call(
+        functools.partial(spread_kernel, devices, whole),
+        out_shape=jax.ShapeDtypeStruct(shape, block.dtype),
+        in_specs=[pl.BlockSpec(memory_space=pltpu.VMEM)],
+        out_specs=pl.BlockSpec(memory_space=pltpu.VMEM),
+        scratch_shapes=[
+            pltpu.SemaphoreType.DMA((devices,)),
+            pltpu.SemaphoreType.DMA((devices,)),
+            pltpu.SemaphoreType.DMA,
+        ],
+        compiler_params=pltpu.CompilerParams(collective_id=number, has_side_effects=True),
+        name="spread%d" % number,
+    )(block)
+
+
+def exchange(blocks, number):
+    return spread(blocks, blocks.shape[0], False, number)
+
+
+def gather(block, devices, number):
+    return spread(block, devices, True, number).reshape(devices * block.shape[0], block.shape[1])
 
 
 def on_device(devices, mask_field, target_print, source_points, source_groups, group_logits, pupil_radius):
@@ -95,8 +159,8 @@
     band = jnp.concatenate(
         [spec[:K, :K] - spec[K:, K:], -(spec[:K, K:] + spec[K:, :K])], 0
     )
-    band = jnp.sum(exchange(band.reshape(devices, 2 * K // devices, K)), 0)
-    band = gather(band, devices)
+    band = jnp.sum(exchange(band.reshape(devices, 2 * K // devices, K), 0), 0)
+    band = gather(band, devices, 1)
 
     kept = jnp.where(passed, band[None], 0.0)
     wide = dot("aq,sqk->sak", lift, kept)
@@ -112,14 +176,14 @@
     image = jnp.sum(share[:, None, None] * bright, 0)
 
     tall = dot("cm,mx->cx", image, up)
-    tall = lax.all_to_all(tall, "slab", 1, 0, tiled=True)
+    tall = exchange(jnp.swapaxes(tall.reshape(cols, devices, rows), 0, 1), 2).reshape(coarse, rows)
     intensity = dot("cx,cy->xy", tall, up)
     resist = jax.nn.sigmoid(steepness * (intensity - threshold))
     misfit = resist - target_print.astype(jnp.float32)
     slope = (2.0 * steepness) * misfit * resist * (1.0 - resist)
     squares = jnp.sum(misfit * misfit)
     down = dot("xy,cy->cx", slope, up)
-    down = lax.all_to_all(down, "slab", 0, 1, tiled=True)
+    down = jnp.swapaxes(exchange(down.reshape(devices, cols, rows), 3), 0, 1).reshape(cols, n)
     pull = dot("cx,mx->cm", down, up)
 
     per_source = jnp.sum(bright * pull[None], (1, 2))
@@ -135,9 +199,9 @@
     grad_band = jnp.sum(jnp.where(passed, settle, 0.0), 0).reshape(devices, 2 * K // devices, K)
     extra = jnp.pad(sums[None, :], ((0, 7), (0, K - sources - 1)))
     extra = jnp.broadcast_to(extra[None], (devices, 8, K))
-    grad_band = jnp.sum(exchange(jnp.concatenate([grad_band, extra], 1)), 0)
+    grad_band = jnp.sum(exchange(jnp.concatenate([grad_band, extra], 1), 4), 0)
     sums = grad_band[-8, : sources + 1]
-    grad_band = gather(grad_band[:-8], devices)
+    grad_band = gather(grad_band[:-8], devices, 5)
     per_source, squares = sums[:-1], sums[-1]
     loss_value = (squares * norming).reshape(1)
     against = jnp.sum(share * per_source)
@@ -146,9 +210,9 @@
 
 
     loc_c2 = jnp.concatenate([loc_c, loc_s], 0)
-    spread = dot("tk,qk->tq", loc_c2, grad_band)
-    spread_re = spread[:rows, :K] - spread[rows:, K:]
-    spread_im = spread[:rows, K:] + spread[rows:, :K]
+    wide_out = dot("tk,qk->tq", loc_c2, grad_band)
+    spread_re = wide_out[:rows, :K] - wide_out[rows:, K:]
+    spread_im = wide_out[:rows, K:] + wide_out[rows:, :K]
     even = dot("xq,yq->xy", jnp.concatenate([spread_re[:, :kh], -spread_im[:, :kh]], 1), fold[0])
     odd = dot("xq,yq->xy", jnp.concatenate([spread_re[:, kh:], -spread_im[:, kh:]], 1), fold[1])
     mask_grad = jnp.concatenate([even + odd, even - odd], 1)

time: 151 us -> 159 us (1.053); the launches traced: 151 us -> 156 us
  Pallas kernels: 0 us -> 97.6 us
  blocking collectives: 88.5 us -> 0 us
  waiting for transfers between devices: 12 us -> 0 us
  starting transfers between devices: 7.41 us -> 0 us
  matrix products: 27.8 us -> 34.8 us
  other arithmetic: 8.98 us -> 15.1 us
  local copies, waits for them, and re-layouts: 2.46 us -> 5.44 us
    pallas_call x0 -> x6, Pallas kernels: none -> 97.6 us  [spread(): pl.pallas_call(functools.partial(spread_kernel, devices, whole), out_shap...]
    all_to_all x3 -> x0, blocking collectives: 46.7 us -> none  [the longest x1 21.1 us: exchange(): return lax.all_to_all(blocks, 'slab', 0, 0)]
    all_gather x2 -> x0, blocking collectives: 41.7 us -> none  [gather(): return lax.all_gather(block, 'slab', tiled=True)]
    all_to_all x1 -> x0, waiting for transfers between devices: 12 us -> none  [exchange(): return lax.all_to_all(blocks, 'slab', 0, 0)]
    all_to_all x1 -> x0, starting transfers between devices: 7.41 us -> none  [exchange(): return lax.all_to_all(blocks, 'slab', 0, 0)]
    dot_general x17, matrix products: 27.8 us -> 34.8 us  [dot(): jnp.einsum(form, left, right, precision=HIGH, preferred_element_type=jnp....]
    reduce_sum x2, other arithmetic: 0.08 us -> 2.83 us  [the longest x1 1.69 us: on_device(): band = jnp.sum(exchange(band.reshape(devices, 2 * K // devices, K), 0), 0)]
  transfers between devices with their start and end apart: 1 -> 0, of which waited for: 1 -> 0; matrix products, arithmetic and copies ran while one was open for 1% -> 0% of each run, Pallas kernels for 0% -> 0%
where the time goes in v3:
time: 159 us; the launch traced here: 156 us
  Pallas kernels  97.6 us (61%)
  matrix products  34.8 us (22%)
  other arithmetic  15.1 us (9%)
  local copies, waits for them, and re-layouts  5.44 us (3%)
  between operations  3.54 us (2%)
    pallas_call x6, Pallas kernels, spread(): pl.pallas_call(functools.partial(spread_kernel, devices, whole), out_shap...  97.6 us
    dot_general x17, matrix products, dot(): jnp.einsum(form, left, right, precision=HIGH, preferred_element_type=jnp....  34.8 us

profile of v3, /device:TPU:0, one launch (start us, length us, event | category | flops | bytes accessed | tf_op | source)
XLA Modules:
  0.0 156.5 jit_solution(7760291497026881688)
XLA Ops:
  1.3 0.8 select_reduce_fusion.1
  2.1 0.6 exponential_reduce_fusion
  2.7 0.7 broadcast_multiply_fusion.1
  3.4 0.7 and_select_fusion
  4.1 0.8 constant_dynamic-slice_fusion
  4.8 0.7 add_multiply_fusion.1
  5.6 0.8 add_multiply_fusion
  6.3 0.8 fusion.58
  7.1 2.0 %fusion.29 = f32[128,256]{1,0:T(8,128)S(1)} fusion(f32[1024,256]{1,0:T(8,128)} %constant.67.clone, f32[128,2048]{1,0:T(8,128)} %param.18), kind=kOutput, calls=%fused_computation.52 | convolution fusion | flops 201457664 | bytes 2228224 | tf_op jit(solution)/shard_map/xy,yq->xq/dot_general | solution.py:23
  9.1 2.0 %fusion.27 = f32[128,256]{1,0:T(8,128)S(1)} fusion(f32[1024,256]{1,0:T(8,128)} %constant.68.clone, f32[128,2048]{1,0:T(8,128)} %param.18), kind=kOutput, calls=%fused_computation.50 | convolution fusion | flops 201457664 | bytes 2228224 | tf_op jit(solution)/shard_map/xy,yq->xq/dot_general | solution.py:23
  11.2 0.6 fusion.37
  11.9 0.8 pad_maximum_fusion.5
  12.7 17.2 %spread0.1 = f32[16,32,256]{2,1,0:T(8,128)} custom-call(f32[16,32,256]{2,1,0:T(8,128)} %bitcast.99), custom_call_target="tpu_custom_call" | custom-call | tf_op jit(solution)/shard_map/spread0/pallas_call | solution.py:93
  29.9 1.7 %reduce_sum.92.in_ref = f32[32,256]{1,0:T(8,128)} reduce(f32[16,32,256]{2,1,0:T(8,128)} %spread0.1, f32[]{:T(128)} %constant.26.clone.1), dimensions={0}, to_apply=%region_2.3 | reduce | flops 122880 | bytes 557060 | tf_op jit(solution)/shard_map/reduce_sum | solution.py:162
  31.6 17.6 %spread1.1 = f32[16,32,256]{2,1,0:T(8,128)} custom-call(f32[32,256]{1,0:T(8,128)} %reduce_sum.92.in_ref), custom_call_target="tpu_custom_call" | custom-call | tf_op jit(solution)/shard_map/spread1/pallas_call | solution.py:93
  49.2 1.2 copy.36
  50.5 4.4 %fusion.1 = f32[16,256,64]{1,2,0:T(8,128)S(1)} fusion(f32[512,256]{0,1:T(8,128)S(1)} %copy.36, s32[]{:T(128)S(6)} %mul.218, s32[16,512]{1,0:T(8,128)S(1)} %add_multiply_fusion, s32[16,256]{1,0:T(8,128)S(1)} %add_multiply_fusion.1, f32[32,256]{1,0:T(8,128)S(1)} %get-tuple-element.21, f32[32,256]{1,0:T(8,128)S(1)} %get-tuple-element.20, ...), kind=kOutput, calls=%fused_computation.2 | convolution fusion | flops 811696128 | bytes 1720324 | tf_op jit(solution)/shard_map/aq,sqk->sak/dot_general | solution.py:23
  55.0 1.9 %fusion.71 = f32[16,2,32,1024]{3,2,1,0:T(8,128)S(1)} fusion(f32[16,2,32,256]{3,2,1,0:T(8,128)S(1)} %bitcast.103, f32[256,1024,1,1]{1,0,3,2:T(8,128)S(1)} %copy-done.5), kind=kOutput, calls=%fused_computation.126 | convolution fusion | flops 1610612736 | bytes 6291456 | tf_op jit(solution)/shard_map/ak,kx->ax/dot_general | solution.py:23
  56.9 1.9 %copy-done = f32[16,2,32,1024]{3,2,1,0:T(8,128)} copy-done((f32[16,2,32,1024]{3,2,1,0:T(8,128)}, f32[16,2,32,1024]{3,2,1,0:T(8,128)S(1)}, u32[]{:S(2)}) %copy-start) | copy-done | bytes 4194328
  58.8 0.5 fusion.20
  59.4 2.7 %convolution_bitcast_fusion.in_ref = f32[16,32,128]{2,1,0:T(8,128)} fusion(f32[16,128,512]{2,1,0:T(8,128)S(1)} %copy-done.3, f32[32,512]{1,0:T(8,128)S(1)} %fusion.20), kind=kOutput, calls=%fused_computation.23 | convolution fusion | flops 201326592 | bytes 4521984 | tf_op jit(solution)/shard_map/cm,mx->cx/dot_general | solution.py:23
  62.1 13.5 %spread2.1 = f32[16,32,128]{2,1,0:T(8,128)} custom-call(f32[16,32,128]{2,1,0:T(8,128)} %convolution_bitcast_fusion.in_ref), custom_call_target="tpu_custom_call" | custom-call | tf_op jit(solution)/shard_map/spread2/pallas_call | solution.py:93
  75.6 4.6 %multiply_reduce_fusion = (f32[]{:T(128)}, f32[128,2048]{1,0:T(8,128)S(1)}) fusion(s32[128,2048]{1,0:T(8,128)S(1)} %copy-done.4, f32[512,128]{1,0:T(8,128)} %bitcast.104, f32[512,2048]{1,0:T(8,128)} %constant.69.clone), kind=kOutput, calls=%fused_computation.36 | convolution fusion | flops 807665664 | bytes 6553604 | tf_op jit(solution)/shard_map/cx,cy->xy/dot_general | solution.py:23
  80.3 2.6 %fusion.22 = f32[512,128]{1,0:T(8,128)} fusion(f32[512,2048]{1,0:T(8,128)S(1)} %copy-done.2, f32[128,2048]{1,0:T(8,128)S(1)} %get-tuple-element.29, s32[128,2048]{1,0:T(8,128)S(1)} %copy-done.4), kind=kOutput, calls=%fused_computation.40 | convolution fusion | flops 806879232 | bytes 6553600 | tf_op jit(solution)/shard_map/xy,cy->cx/dot_general | solution.py:23
  82.8 12.2 %spread3.1 = f32[16,32,128]{2,1,0:T(8,128)} custom-call(f32[16,32,128]{2,1,0:T(8,128)} %bitcast.102), custom_call_target="tpu_custom_call" | custom-call | tf_op jit(solution)/shard_map/spread3/pallas_call | solution.py:93
  95.0 4.3 %fusion.52 = f32[32,512]{1,0:T(8,128)S(1)} fusion(f32[512,2048]{1,0:T(8,128)} %constant.69.clone, f32[16,32,128]{2,1,0:T(8,128)} %spread3.1), kind=kOutput, calls=%fused_computation.78 | convolution fusion | flops 201326592 | bytes 4521984 | tf_op jit(solution)/shard_map/cx,mx->cm/dot_general | solution.py:23
  99.3 0.4 fusion.21
  99.8 0.6 multiply_multiply_fusion.1
  100.4 0.7 maximum_bitcast_fusion.3
  101.2 1.0 fusion.13
  102.2 1.0 fusion.14
  103.4 4.6 %fusion = f32[512,256]{0,1:T(8,128)S(1)} fusion(s32[]{:T(128)S(6)} %mul.218, s32[16,512]{1,0:T(8,128)S(1)} %add_multiply_fusion, s32[16,256]{1,0:T(8,128)S(1)} %add_multiply_fusion.1, f32[16,32,256]{2,1,0:T(8,128)S(1)} %fusion.23, f32[16,32,256]{2,1,0:T(8,128)S(1)} %fusion.25, f32[32,256]{1,0:T(8,128)S(1)} %get-tuple-element.21, ...), kind=kOutput, calls=%fused_computation.1 | convolution fusion | flops 813924352 | bytes 1720324 | tf_op jit(solution)/shard_map/aq,sak->sqk/dot_general | solution.py:23
  108.0 0.2 copy.41
  108.2 0.9 pad_maximum_fusion.4.in_ref
  109.1 18.9 %spread4.1 = f32[16,40,256]{2,1,0:T(8,128)} custom-call(f32[16,40,256]{2,1,0:T(8,128)} %pad_maximum_fusion.4.in_ref), custom_call_target="tpu_custom_call" | custom-call | tf_op jit(solution)/shard_map/spread4/pallas_call | solution.py:93
  128.0 1.1 reduce_sum.97
  129.1 0.6 multiply_reduce_fusion.1
  129.7 0.6 slice.179
  131.0 0.7 subtract_multiply_fusion.2
  131.6 0.6 slice.180.in_ref
  132.4 0.5 broadcast_multiply_fusion
  132.9 18.3 %spread5.1 = f32[16,32,256]{2,1,0:T(8,128)} custom-call(f32[32,256]{1,0:T(8,128)} %slice.180.in_ref), custom_call_target="tpu_custom_call" | custom-call | tf_op jit(solution)/shard_map/spread5/pallas_call | solution.py:93
  151.1 1.5 fusion.48
  152.7 0.4 fusion.53
  153.1 0.4 convolution_add_fusion.1
  153.5 0.4 fusion.55
  153.9 0.4 fusion.68
  154.3 1.0 pad_maximum_fusion.3
  (39 shorter events, 0.5 us)
Async XLA Ops:
  0.6 10.5 %copy-start.12 = (f32[128,256]{1,0:T(8,128)S(1)}, f32[128,256]{1,0:T(8,128)}, u32[]{:S(2)}) copy-start(f32[128,256]{1,0:T(8,128)} %constant.73.clone) | copy-start | bytes 393220
  0.6 10.5 %copy-start.13 = (f32[128,256]{1,0:T(8,128)S(1)}, f32[128,256]{1,0:T(8,128)}, u32[]{:S(2)}) copy-start(f32[128,256]{1,0:T(8,128)} %constant.72.clone) | copy-start | bytes 393220
  50.5 4.5 %copy-start.5 = (f32[256,1024,1,1]{1,0,3,2:T(8,128)S(1)}, f32[256,1024,1,1]{1,0,3,2:T(8,128)}, u32[]{:S(2)}) copy-start(f32[256,1024,1,1]{1,0,3,2:T(8,128)} %constant.90) | copy-start | bytes 3145732
  54.9 4.4 %copy-start.3 = (f32[16,128,512]{2,1,0:T(8,128)S(1)}, f32[16,128,512]{2,1,0:T(8,128)}, u32[]{:S(2)}) copy-start(f32[16,128,512]{2,1,0:T(8,128)} %constant.83) | copy-start | bytes 12582916
  56.9 1.9 %copy-start = (f32[16,2,32,1024]{3,2,1,0:T(8,128)}, f32[16,2,32,1024]{3,2,1,0:T(8,128)S(1)}, u32[]{:S(2)}) copy-start(f32[16,2,32,1024]{3,2,1,0:T(8,128)S(1)} %fusion.71) | copy-start | bytes 12582916
  58.8 16.8 %copy-start.4 = (s32[128,2048]{1,0:T(8,128)S(1)}, s32[128,2048]{1,0:T(8,128)}, u32[]{:S(2)}) copy-start(s32[128,2048]{1,0:T(8,128)} %param.19) | copy-start | bytes 3145732
  75.6 4.6 %copy-start.2 = (f32[512,2048]{1,0:T(8,128)S(1)}, f32[512,2048]{1,0:T(8,128)}, u32[]{:S(2)}) copy-start(f32[512,2048]{1,0:T(8,128)} %constant.69.clone) | copy-start | bytes 12582916
  95.0 4.3 %copy-start.1 = (f32[16,2,32,1024]{3,2,1,0:T(8,128)S(1)}, f32[16,2,32,1024]{3,2,1,0:T(8,128)}, u32[]{:S(2)}) copy-start(f32[16,2,32,1024]{3,2,1,0:T(8,128)} %copy-done) | copy-start | bytes 12582916
  99.8 1.4 copy-start.8
  99.8 2.4 %copy-start.7 = (f32[256,512,1,1]{1,0,3,2:T(8,128)S(1)}, f32[256,512,1,1]{1,0,3,2:T(8,128)}, u32[]{:S(2)}) copy-start(f32[256,512,1,1]{1,0,3,2:T(8,128)} %constant.91) | copy-start | bytes 1572868
  108.0 24.3 %copy-start.14 = (s32[16]{0:T(128)S(1)}, s32[16]{0:T(128)}, u32[]{:S(2)}) copy-start(s32[16]{0:T(128)} %param.21) | copy-start | bytes 196
  108.0 44.7 %copy-start.10 = (f32[1024,128]{1,0:T(8,128)S(1)}, f32[1024,128]{1,0:T(8,128)}, u32[]{:S(2)}) copy-start(f32[1024,128]{1,0:T(8,128)} %constant.88) | copy-start | bytes 1572868
  108.0 45.1 %copy-start.6 = (f32[1024,128]{1,0:T(8,128)S(1)}, f32[1024,128]{1,0:T(8,128)}, u32[]{:S(2)}) copy-start(f32[1024,128]{1,0:T(8,128)} %constant.89) | copy-start | bytes 1572868
  108.2 45.2 %copy-start.9 = (f32[1024,128]{1,0:T(8,128)S(1)}, f32[1024,128]{1,0:T(8,128)}, u32[]{:S(2)}) copy-start(f32[1024,128]{1,0:T(8,128)} %constant.86) | copy-start | bytes 1572868
  109.1 44.7 %copy-start.11 = (f32[1024,128]{1,0:T(8,128)S(1)}, f32[1024,128]{1,0:T(8,128)}, u32[]{:S(2)}) copy-start(f32[1024,128]{1,0:T(8,128)} %constant.87) | copy-start | bytes 1572868
